TPU v7x, 32 devices: a whole 2x2x4 slice. The times are simulated.
32 devices in a mesh: seq: 16 (over z, x, core), fsdp: 2 (over y).
Axes of the slice: x: 2, y: 2, z: 4, core: 2. Of those that a mesh axis runs over, the one named last changes fastest.
Arguments:
- prompt: bfloat16 [2, 256, 4096], P('fsdp'), may hold values from -6 to 6
- lengths: int32 [2], P('fsdp'), may hold values from 1 to 256, 384 in all
- timesteps: int32 [2], P('fsdp'), may hold values from 0 to 999
- ref_errors: float32 [2, 2], P('fsdp'), may hold values from 4.2 to 4.45
- gain_ffn: float32 [4096], replicated, may hold values from 0.5 to 1.5
- w_in_gate: bfloat16 [4096, 8192], P('fsdp', 'seq'), may hold values from -0.09375 to 0.09375
- w_in_up: bfloat16 [4096, 8192], P('fsdp', 'seq'), may hold values from -0.09375 to 0.09375
- w_in_down: bfloat16 [8192, 4096], P('seq', 'fsdp'), may hold values from -0.0625 to 0.0625
- gain_final: float32 [4096], replicated, may hold values from 0.5 to 1.5
- w_context: bfloat16 [4096, 2048], P('fsdp', 'seq'), may hold values from -0.09375 to 0.09375
- image_q: bfloat16 [2, 2, 1024, 1024], P('fsdp', None, 'seq'), may hold values from -128 to 128
- image_k: bfloat16 [2, 2, 1024, 1024], P('fsdp', None, 'seq'), may hold values from -4 to 4
- image_v: bfloat16 [2, 2, 1024, 1024], P('fsdp', None, 'seq'), may hold values from -6 to 6
- w_out: bfloat16 [1024, 1280], P('fsdp'), may hold values from -0.1875 to 0.1875
- target: bfloat16 [2, 2, 1024, 1280], P('fsdp', None, 'seq'), may hold values from -12 to 12
Outputs:
- pair_loss: float32 [2], P('fsdp')
- grad_q: bfloat16 [2, 2, 1024, 1024], P('fsdp', None, None, 'seq')
- grad_k: bfloat16 [2, 2, 1024, 1024], P('fsdp', None, None, 'seq')
- grad_v: bfloat16 [2, 2, 1024, 1024], P('fsdp', None, None, 'seq')
All inputs are finite; a program needn't handle non-finite values. No bound on the sum of `lengths` on one device may be relied on, other than what follows from the above.
Results may differ from a plain program's by a relative error of at most 0.029.
Values may be sent and summed in bfloat16 or wider, within the bound.
No kernel may reach another device: no remote copies, remote signals or barrier semaphores. Data moves between devices by JAX's collectives and lax.ppermute only.
A program may use at most 128 MiB of HBM per device.

v0:
```python
import math
import jax
import jax.numpy as jnp
from jax import lax
from jax.sharding import PartitionSpec as P

PROMPT = 256
HEAD = 64
CH = 1280
dpo_beta = 20.0
norm_eps = 1e-06


def rms_gain(values, gain):
    mean_sq = jnp.mean(values * values, axis=-1, keepdims=True)
    return values * lax.rsqrt(mean_sq + norm_eps) * gain


def noise_level(step_index):
    fraction = (step_index.astype(jnp.float32) + 1.0) / 1000.0
    return 3.0 * fraction / (1.0 + 2.0 * fraction)


def softmax_rows(queries, key_rows, key_mask):
    scores = jnp.einsum("qh,kh->qk", queries, key_rows, preferred_element_type=jnp.float32) * (
        1.0 / math.sqrt(HEAD)
    )
    scores = jnp.where(key_mask[None, :], scores, -jnp.inf)
    top_score = jnp.max(scores, axis=-1, keepdims=True)
    weights = jnp.exp(scores - top_score)
    return (weights / jnp.sum(weights, axis=-1, keepdims=True)).astype(jnp.bfloat16)


def stream_forward(queries, key_rows, value_rows, key_mask):
    seq_len = queries.shape[0]
    block_rows = min(512, seq_len)
    query_blocks = queries.reshape(seq_len // block_rows, block_rows, HEAD)

    def one_block(query_block):
        probs_bf = softmax_rows(query_block, key_rows, key_mask)
        return jnp.dot(probs_bf, value_rows, preferred_element_type=jnp.float32).astype(
            jnp.bfloat16
        )

    return lax.map(one_block, query_blocks).reshape(seq_len, HEAD)


def stream_backward(queries, key_rows, value_rows, key_mask, attended, grad_out):
    seq_len = queries.shape[0]
    block_rows = min(512, seq_len)
    block_count = seq_len // block_rows

    def one_block(carried, pieces):
        key_acc, value_acc = carried
        query_block, out_block, grad_block = pieces
        probs_bf = softmax_rows(query_block, key_rows, key_mask)
        grad_prob = jnp.einsum(
            "qh,kh->qk", grad_block, value_rows, preferred_element_type=jnp.float32
        )
        row_delta = jnp.sum(
            grad_block.astype(jnp.float32) * out_block.astype(jnp.float32), axis=-1, keepdims=True
        )
        grad_score = (
            probs_bf.astype(jnp.float32) * (grad_prob - row_delta) * (1.0 / math.sqrt(HEAD))
        ).astype(jnp.bfloat16)
        grad_query = jnp.dot(grad_score, key_rows, preferred_element_type=jnp.float32).astype(
            jnp.bfloat16
        )
        key_acc = key_acc + jnp.einsum(
            "qk,qh->kh", grad_score[:, :seq_len], query_block, preferred_element_type=jnp.float32
        )
        value_acc = value_acc + jnp.einsum(
            "qk,qh->kh", probs_bf[:, :seq_len], grad_block, preferred_element_type=jnp.float32
        )
        return ((key_acc, value_acc), grad_query)

    zeros_acc = jnp.zeros((seq_len, HEAD), jnp.float32)
    shaped = (
        queries.reshape(block_count, block_rows, HEAD),
        attended.reshape(block_count, block_rows, HEAD),
        grad_out.reshape(block_count, block_rows, HEAD),
    )
    (key_acc, value_acc), grad_query = lax.scan(one_block, (zeros_acc, zeros_acc), shaped)
    return (
        grad_query.reshape(seq_len, HEAD),
        key_acc.astype(jnp.bfloat16),
        value_acc.astype(jnp.bfloat16),
    )


def on_device(
    prompt,
    lengths,
    timesteps,
    ref_errors,
    gain_ffn,
    w_in_gate,
    w_in_up,
    w_in_down,
    gain_final,
    w_context,
    image_q,
    image_k,
    image_v,
    w_out,
    target,
):
    gate_full, up_full, down_full, context_full, out_full = (
        lax.all_gather(w_in_gate, "fsdp", axis=0, tiled=True),
        lax.all_gather(w_in_up, "fsdp", axis=0, tiled=True),
        lax.all_gather(w_in_down, "fsdp", axis=1, tiled=True),
        lax.all_gather(w_context, "fsdp", axis=0, tiled=True),
        lax.all_gather(w_out, "fsdp", axis=0, tiled=True),
    )
    prompt_f32 = prompt[0].astype(jnp.float32)
    normed = rms_gain(prompt_f32, gain_ffn).astype(jnp.bfloat16)
    gate_act = jnp.dot(normed, gate_full, preferred_element_type=jnp.float32)
    up_act = jnp.dot(normed, up_full, preferred_element_type=jnp.float32)
    hidden = (jax.nn.gelu(gate_act, approximate=True) * up_act).astype(jnp.bfloat16)
    partial_value = jnp.dot(hidden, down_full, preferred_element_type=jnp.float32)
    summed = lax.psum(partial_value.astype(jnp.bfloat16), "seq").astype(jnp.float32)
    encoded = rms_gain(prompt_f32 + summed, gain_final).astype(jnp.bfloat16)
    context = jnp.dot(encoded, context_full, preferred_element_type=jnp.float32).astype(
        jnp.bfloat16
    )
    text_keys = context[:, :HEAD]
    text_values = context[:, HEAD:]
    q_heads, k_heads, v_heads = (
        lax.all_to_all(image_q, "seq", split_axis=3, concat_axis=2, tiled=True),
        lax.all_to_all(image_k, "seq", split_axis=3, concat_axis=2, tiled=True),
        lax.all_to_all(image_v, "seq", split_axis=3, concat_axis=2, tiled=True),
    )
    seq_len = q_heads.shape[2]
    key_mask = jnp.arange(seq_len + PROMPT) < seq_len + lengths[0]
    key_sets = []
    value_sets = []
    head_outs = []
    for stream in range(2):
        key_rows = jnp.concatenate([k_heads[0, stream], text_keys], axis=0)
        value_rows = jnp.concatenate([v_heads[0, stream], text_values], axis=0)
        key_sets.append(key_rows)
        value_sets.append(value_rows)
        head_outs.append(stream_forward(q_heads[0, stream], key_rows, value_rows, key_mask))
    attended = jnp.stack(head_outs)[None]
    tok_out = lax.all_to_all(attended, "seq", split_axis=2, concat_axis=3, tiled=True)
    predicted = jnp.einsum("sti,ic->stc", tok_out[0], out_full, preferred_element_type=jnp.float32)
    residual = predicted - target[0].astype(jnp.float32)
    partial_err = jnp.sum(residual * residual, axis=(1, 2))
    error_sums = lax.psum(partial_err, "seq")
    mean_errors = error_sums / (seq_len * CH)
    error_gap = mean_errors[0] - ref_errors[0, 0] - (mean_errors[1] - ref_errors[0, 1])
    sigma_t = noise_level(timesteps[0])
    logit_value = dpo_beta * sigma_t * error_gap
    pair_loss = jax.nn.softplus(logit_value)[None]
    coefficient = sigma_t * jax.nn.sigmoid(logit_value)
    stream_signs = jnp.stack([coefficient, -coefficient])
    grad_pred = (stream_signs[:, None, None] * residual).astype(jnp.bfloat16)
    grad_tok = jnp.einsum(
        "stc,ic->sti", grad_pred, out_full, preferred_element_type=jnp.float32
    ).astype(jnp.bfloat16)
    grad_heads = lax.all_to_all(grad_tok[None], "seq", split_axis=3, concat_axis=2, tiled=True)
    query_grads = []
    key_grads = []
    value_grads = []
    for stream in range(2):
        grad_query, grad_key, grad_value = stream_backward(
            q_heads[0, stream],
            key_sets[stream],
            value_sets[stream],
            key_mask,
            head_outs[stream],
            grad_heads[0, stream],
        )
        query_grads.append(grad_query)
        key_grads.append(grad_key)
        value_grads.append(grad_value)
    return (
        pair_loss,
        jnp.stack(query_grads)[None],
        jnp.stack(key_grads)[None],
        jnp.stack(value_grads)[None],
    )


def solution(mesh):
    return jax.shard_map(
        on_device,
        mesh=mesh,
        in_specs=(
            P("fsdp", None, None),
            P("fsdp"),
            P("fsdp"),
            P("fsdp", None),
            P(),
            P("fsdp", "seq"),
            P("fsdp", "seq"),
            P("seq", "fsdp"),
            P(),
            P("fsdp", "seq"),
            P("fsdp", None, "seq", None),
            P("fsdp", None, "seq", None),
            P("fsdp", None, "seq", None),
            P("fsdp", None),
            P("fsdp", None, "seq", None),
        ),
        out_specs=(
            P("fsdp"),
            P("fsdp", None, None, "seq"),
            P("fsdp", None, None, "seq"),
            P("fsdp", None, None, "seq"),
        ),
        check_vma=False,
    )
```

profile of v0, /device:TPU:0, one launch (start us, length us, event | category | flops | bytes accessed | tf_op | source)
XLA Modules:
  0.0 485.4 jit_solution(12774204976036497098)
XLA Ops:
  10.0 59.0 %all-gather.6.cloned.1.call-done = bf16[4096,512]{1,0:T(8,128)(2,1)} async-done(((bf16[2048,512]{1,0:T(8,128)(2,1)}), bf16[4096,512]{1,0:T(8,128)(2,1)}) %all-gather.6.cloned.1.call-update) | async-done | bytes 4194320 | tf_op jit(solution)/shard_map/all_gather | solution.py:109
  69.0 3.6 fusion.102
  72.6 54.7 %all-gather.10.cloned.1.call-done = bf16[512,4096]{1,0:T(8,128)(2,1)} async-done(((bf16[512,2048]{1,0:T(8,128)(2,1)}), bf16[512,4096]{1,0:T(8,128)(2,1)}) %all-gather.10.cloned.1.call-update) | async-done | bytes 4194320 | tf_op jit(solution)/shard_map/all_gather | solution.py:111
  127.3 58.3 %all-gather.8.cloned.1.call-done = bf16[4096,512]{1,0:T(8,128)(2,1)} async-done(((bf16[2048,512]{1,0:T(8,128)(2,1)}), bf16[4096,512]{1,0:T(8,128)(2,1)}) %all-gather.8.cloned.1.call-update) | async-done | bytes 4194320 | tf_op jit(solution)/shard_map/all_gather | solution.py:110
  185.6 7.3 %convolution_convert_fusion.2 = bf16[256,4096]{1,0:T(8,128)(2,1)} fusion(bf16[512,4096]{1,0:T(8,128)(2,1)} %all-gather.10.cloned.1.call-done, f32[256,512]{1,0:T(8,128)S(1)} %fusion.102, bf16[4096,512]{1,0:T(8,128)(2,1)} %all-gather.8.cloned.1.call-done, bf16[1,256,4096]{2,1,0:T(8,128)(2,1)S(1)} %copy-done.4, f32[4096]{0:T(1024)S(1)} %copy-done.15, ...), kind=kOutput, calls=%fused_computation.97 | convolution fusion | flops 2152988672 | bytes 13124608 | tf_op jit(solution)/shard_map/dot_general | solution.py:120
  195.4 5.6 %all-to-all-start.2 = ((bf16[16,2,4096]{2,1,0:T(2,128)(2,1)}), bf16[16,2,4096]{2,1,0:T(2,128)(2,1)S(1)}, u32[]{:S(2)}, u32[]{:S(2)}) async-start(bf16[16,2,4096]{2,1,0:T(2,128)(2,1)} %reshape.73), calls=%async_computation.2 | async-start | bytes 524288 | tf_op jit(solution)/shard_map/all_to_all | solution.py:131
  202.5 11.2 %all-to-all-done.2 = bf16[16,2,4096]{2,1,0:T(2,128)(2,1)S(1)} async-done(((bf16[16,2,4096]{2,1,0:T(2,128)(2,1)}), bf16[16,2,4096]{2,1,0:T(2,128)(2,1)S(1)}, u32[]{:S(2)}, u32[]{:S(2)}) %all-to-all-start.2) | async-done | bytes 262176 | tf_op jit(solution)/shard_map/all_to_all | solution.py:131
  213.7 3.5 all-to-all-start.1
  219.7 10.4 %all-to-all-done.1 = bf16[16,2,4096]{2,1,0:T(2,128)(2,1)S(1)} async-done(((bf16[16,2,4096]{2,1,0:T(2,128)(2,1)}), bf16[16,2,4096]{2,1,0:T(2,128)(2,1)S(1)}, u32[]{:S(2)}, u32[]{:S(2)}) %all-to-all-start.1) | async-done | bytes 262176 | tf_op jit(solution)/shard_map/all_to_all | solution.py:130
  230.1 4.2 all-to-all-start
  236.4 2.2 reshape.72
  241.4 4.5 all-to-all-done
  249.1 50.5 %all-reduce.2.cloned.1.call-done = bf16[256,4096]{1,0:T(8,128)(2,1)} async-done(((bf16[256,4096]{1,0:T(8,128)(2,1)}), bf16[256,4096]{1,0:T(8,128)(2,1)}) %all-reduce.2.cloned.1.call-update) | async-done | bytes 2097168 | tf_op jit(solution)/shard_map/psum | solution.py:121
  299.6 2.4 multiply_reduce_fusion
  302.0 19.6 %all-gather.12.cloned.1.call-done = bf16[4096,128]{1,0:T(8,128)(2,1)} async-done(((bf16[2048,128]{1,0:T(8,128)(2,1)}), bf16[4096,128]{1,0:T(8,128)(2,1)}) %all-gather.12.cloned.1.call-update) | async-done | bytes 1048592 | tf_op jit(solution)/shard_map/all_gather | solution.py:112
  321.6 3.0 fusion.91
  326.7 6.9 %while.52 = (s32[]{:T(128)}, bf16[2,512,64]{1,2,0:T(8,128)(2,1)}, bf16[2,512,64]{2,1,0:T(8,128)(2,1)}, bf16[1280,64]{1,0:T(8,128)(2,1)S(1)}, bf16[1280,64]{1,0:T(8,128)(2,1)S(1)}, /*index=5*/s32[]{:T(128)}, s32[]{:T(128)}) while((s32[]{:T(128)}, bf16[2,512,64]{1,2,0:T(8,128)(2,1)}, bf16[2,512,64]{2,1,0:T(8,128)(2,1)}, ...), condition=%wide.region_6.7_spmd.clone, body=%wide.region_3.6_spmd.clone.sunk | while | flops 173048064 | bytes 8402513 | solution.py:45
  334.8 3.9 while.53
  340.5 5.6 %all-to-all-start.3 = ((bf16[16,2,4096]{2,1,0:T(2,128)(2,1)}), bf16[16,2,4096]{2,1,0:T(2,128)(2,1)S(1)}, u32[]{:S(2)}, u32[]{:S(2)}) async-start(bf16[16,2,4096]{2,1,0:T(2,128)(2,1)} %reshape.75), calls=%async_computation.3 | async-start | bytes 524288 | tf_op jit(solution)/shard_map/all_to_all | solution.py:145
  347.5 8.7 %all-to-all-done.3 = bf16[16,2,4096]{2,1,0:T(2,128)(2,1)S(1)} async-done(((bf16[16,2,4096]{2,1,0:T(2,128)(2,1)}), bf16[16,2,4096]{2,1,0:T(2,128)(2,1)S(1)}, u32[]{:S(2)}, u32[]{:S(2)}) %all-to-all-start.3) | async-done | bytes 262176 | tf_op jit(solution)/shard_map/all_to_all | solution.py:145
  357.9 4.1 all-gather.14.cloned.1.call-done
  362.0 3.4 multiply_reduce_fusion.1
  365.4 33.0 %psum.15 = f32[2]{0:T(128)S(1)} all-reduce(f32[2]{0:T(128)S(1)} %get-tuple-element.468), channel_id=1, replica_groups=mesh['seq'=16,'fsdp'=2] {'seq'}, use_global_device_ids=true, to_apply=%region_12.13 | all-reduce | flops 2 | bytes 16 | tf_op jit(solution)/shard_map/psum | solution.py:149
  401.7 2.8 fusion.88
  406.8 3.8 all-to-all-start.4
  410.7 9.6 %all-to-all-done.4 = bf16[16,2,4096]{2,1,0:T(2,128)(2,1)S(1)} async-done(((bf16[16,2,4096]{2,1,0:T(2,128)(2,1)}), bf16[16,2,4096]{2,1,0:T(2,128)(2,1)S(1)}, u32[]{:S(2)}, u32[]{:S(2)}) %all-to-all-start.4) | async-done | bytes 262176 | tf_op jit(solution)/shard_map/all_to_all | solution.py:161
  423.6 22.8 %while.54 = (s32[]{:T(128)}, f32[1024,64]{0,1:T(8,128)}, f32[1024,64]{0,1:T(8,128)}, bf16[2,512,64]{1,2,0:T(8,128)(2,1)}, bf16[2,512,64]{2,1,0:T(8,128)(2,1)}, /...) while((s32[]{:T(128)}, f32[1024,64]{0,1:T(8,128)}, ...), condition=%wide.region_17.18_spmd.clone, body=%wide.region_13.17_spmd.clone.sunk | while | flops 394821376 | bytes 17910924 | solution.py:83
  432.9 1.9 convolution_add_fusion.9
  441.1 2.1 convolution_add_fusion.8
  444.3 2.1 convolution_add_fusion.9
  450.4 18.9 %while.55 = (s32[]{:T(128)}, f32[1024,64]{0,1:T(8,128)}, f32[1024,64]{0,1:T(8,128)}, bf16[2,512,64]{1,2,0:T(8,128)(2,1)}, bf16[2,512,64]{2,1,0:T(8,128)(2,1)S(1)...) while((s32[]{:T(128)}, f32[1024,64]{0,1:T(8,128)}, ...), condition=%wide.region_22.23_spmd.clone, body=%wide.region_18.22_spmd.clone.sunk | while | flops 394821376 | bytes 21187588 | solution.py:83
  464.1 2.0 convolution_add_fusion.10
  (175 shorter events, 86.3 us)
Async XLA Ops:
  7.2 2.3 copy-start.4
  7.2 61.8 %all-gather.6.cloned.1.call-start = ((), (), s32[]{:S(2)}) async-start(), calls=%async_computation.5 | async-start | bytes 6291456 | tf_op jit(solution)/shard_map/all_gather | solution.py:109
  7.9 119.4 %all-gather.10.cloned.1.call-start = ((), (), s32[]{:S(2)}) async-start(), calls=%async_computation.7 | async-start | bytes 6291456 | tf_op jit(solution)/shard_map/all_gather | solution.py:111
  8.7 60.4 %copy-start.15 = (f32[4096]{0:T(1024)S(1)}, f32[4096]{0:T(1024)}, u32[]{:S(2)}) copy-start(f32[4096]{0:T(1024)} %param.27) | copy-start | bytes 49156
  8.7 176.9 %all-gather.8.cloned.1.call-start = ((), (), s32[]{:S(2)}) async-start(), calls=%async_computation.6 | async-start | bytes 6291456 | tf_op jit(solution)/shard_map/all_gather | solution.py:110
  9.4 290.2 %all-reduce.2.cloned.1.call-start = ((), (), s32[]{:S(2)}) async-start(), calls=%async_computation.8 | async-start | bytes 4194304 | tf_op jit(solution)/shard_map/psum | solution.py:121
  193.0 0.9 copy-start.10
  193.0 8.1 %copy-start.11 = (bf16[1,2,64,1024]{3,2,1,0:T(8,128)(2,1)S(1)}, bf16[1,2,64,1024]{3,2,1,0:T(8,128)(2,1)}, u32[]{:S(2)}) copy-start(bf16[1,2,64,1024]{3,2,1,0:T(8,128)(2,1)} %param.34) | copy-start | bytes 786436
  193.0 128.6 %all-gather.12.cloned.1.call-start = ((), (), s32[]{:S(2)}) async-start(), calls=%async_computation.9 | async-start | bytes 1572864 | tf_op jit(solution)/shard_map/all_gather | solution.py:112
  195.4 18.3 %all-to-all-start.2 = ((bf16[16,2,4096]{2,1,0:T(2,128)(2,1)}), bf16[16,2,4096]{2,1,0:T(2,128)(2,1)S(1)}, u32[]{:S(2)}, u32[]{:S(2)}) async-start(bf16[16,2,4096]{2,1,0:T(2,128)(2,1)} %reshape.73), calls=%async_computation.2 | async-start | bytes 524288 | tf_op jit(solution)/shard_map/all_to_all | solution.py:131
  213.7 16.3 %all-to-all-start.1 = ((bf16[16,2,4096]{2,1,0:T(2,128)(2,1)}), bf16[16,2,4096]{2,1,0:T(2,128)(2,1)S(1)}, u32[]{:S(2)}, u32[]{:S(2)}) async-start(bf16[16,2,4096]{2,1,0:T(2,128)(2,1)} %reshape.71), calls=%async_computation.1 | async-start | bytes 524288 | tf_op jit(solution)/shard_map/all_to_all | solution.py:130
  230.1 5.4 %copy-start.7 = (bf16[16,2,4096]{2,1,0:T(2,128)(2,1)}, bf16[16,2,4096]{2,1,0:T(2,128)(2,1)S(1)}, u32[]{:S(2)}) copy-start(bf16[16,2,4096]{2,1,0:T(2,128)(2,1)S(1)} %all-to-all-done.1) | copy-start | bytes 786436
  230.1 15.9 %all-to-all-start = ((bf16[16,2,4096]{2,1,0:T(2,128)(2,1)}), bf16[16,2,4096]{2,1,0:T(2,128)(2,1)}, u32[]{:S(2)}, u32[]{:S(2)}) async-start(bf16[16,2,4096]{2,1,0:T(2,128)(2,1)} %reshape.69), calls=%async_computation | async-start | bytes 524288 | tf_op jit(solution)/shard_map/all_to_all | solution.py:129
  234.3 127.7 %all-gather.14.cloned.1.call-start = ((), (), s32[]{:S(2)}) async-start(), calls=%async_computation.10 | async-start | bytes 3932160 | tf_op jit(solution)/shard_map/all_gather | solution.py:113
  248.0 73.5 %copy-start.16 = (f32[4096]{0:T(1024)S(1)}, f32[4096]{0:T(1024)}, u32[]{:S(2)}) copy-start(f32[4096]{0:T(1024)} %param.31) | copy-start | bytes 49156
  301.9 22.9 %copy-start.8 = (bf16[1024,64]{1,0:T(8,128)(2,1)S(1)}, bf16[1024,64]{1,0:T(8,128)(2,1)}, u32[]{:S(2)}) copy-start(bf16[1024,64]{1,0:T(8,128)(2,1)} %get-tuple-element.451) | copy-start | bytes 393220
  301.9 22.9 %copy-start.9 = (bf16[1024,64]{1,0:T(8,128)(2,1)S(1)}, bf16[1024,64]{1,0:T(8,128)(2,1)}, u32[]{:S(2)}) copy-start(bf16[1024,64]{1,0:T(8,128)(2,1)} %get-tuple-element.452) | copy-start | bytes 393220
  333.6 1.3 copy-start.3
  338.7 19.2 %copy-start.1 = (bf16[1280,64]{1,0:T(8,128)(2,1)}, bf16[1280,64]{1,0:T(8,128)(2,1)S(1)}, u32[]{:S(2)}) copy-start(bf16[1280,64]{1,0:T(8,128)(2,1)S(1)} %get-tuple-element.807) | copy-start | bytes 491524
  338.7 19.2 %copy-start.5 = (bf16[2,512,64]{1,2,0:T(8,128)(2,1)}, bf16[2,512,64]{1,2,0:T(8,128)(2,1)S(1)}, u32[]{:S(2)}) copy-start(bf16[2,512,64]{1,2,0:T(8,128)(2,1)S(1)} %get-tuple-element.734) | copy-start | bytes 393220
  338.7 8.1 %copy-start.14 = (f32[1,2]{1,0:T(1,128)S(1)}, f32[1,2]{1,0:T(1,128)}, u32[]{:S(2)}) copy-start(f32[1,2]{1,0:T(1,128)} %param.26) | copy-start | bytes 28
  340.5 15.6 %all-to-all-start.3 = ((bf16[16,2,4096]{2,1,0:T(2,128)(2,1)}), bf16[16,2,4096]{2,1,0:T(2,128)(2,1)S(1)}, u32[]{:S(2)}, u32[]{:S(2)}) async-start(bf16[16,2,4096]{2,1,0:T(2,128)(2,1)} %reshape.75), calls=%async_computation.3 | async-start | bytes 524288 | tf_op jit(solution)/shard_map/all_to_all | solution.py:145
  362.0 39.7 %copy-start = (bf16[1024,1280]{1,0:T(8,128)(2,1)S(1)}, bf16[1024,1280]{1,0:T(8,128)(2,1)}, u32[]{:S(2)}) copy-start(bf16[1024,1280]{1,0:T(8,128)(2,1)} %all-gather.14.cloned.1.call-done) | copy-start | bytes 7864324
  406.8 13.5 %all-to-all-start.4 = ((bf16[16,2,4096]{2,1,0:T(2,128)(2,1)}), bf16[16,2,4096]{2,1,0:T(2,128)(2,1)S(1)}, u32[]{:S(2)}, u32[]{:S(2)}) async-start(bf16[16,2,4096]{2,1,0:T(2,128)(2,1)} %reshape.77), calls=%async_computation.4 | async-start | bytes 524288 | tf_op jit(solution)/shard_map/all_to_all | solution.py:161
  451.5 0.9 copy-start.6
  451.5 2.1 copy-start.2
  455.1 2.2 copy-start.12
  458.6 0.7 copy-start.13
  460.5 0.9 copy-start.6
  460.5 2.1 copy-start.2
  464.1 3.2 copy-start.12
  468.5 0.7 copy-start.13
Sparse Core Ops, SparseCore 0:
  9.5 59.4 all-gather.5
  70.5 56.7 all-gather.9
  128.9 56.7 all-gather.7
  193.1 106.4 all-reduce.1
  301.0 20.5 all-gather.11
  323.0 38.9 all-gather.13
where the time goes:
time: 487 us; the launch traced here: 485 us
  waiting for transfers between devices  294 us (60%)
  matrix products  57.2 us (12%)
  local copies, waits for them, and re-layouts  36 us (7%)
  blocking collectives  33 us (7%)
  starting transfers between devices  23.1 us (5%)
  other arithmetic  22.4 us (5%)
  between operations  19.8 us (4%)
    all_gather x1, waiting for transfers between devices, on_device(): lax.all_gather(w_in_gate, 'fsdp', axis=0, tiled=True)  59 us
    all_gather x1, waiting for transfers between devices, on_device(): lax.all_gather(w_in_up, 'fsdp', axis=0, tiled=True)  58.3 us
    all_gather x1, waiting for transfers between devices, on_device(): lax.all_gather(w_in_down, 'fsdp', axis=1, tiled=True)  54.7 us
    psum x1, waiting for transfers between devices, on_device(): lax.psum(partial_value.astype(jnp.bfloat16), 'seq').astype(jnp.float32)  50.5 us
    psum x1, blocking collectives, on_device(): error_sums = lax.psum(partial_err, 'seq')  33 us
    all_gather x1, waiting for transfers between devices, on_device(): lax.all_gather(w_context, 'fsdp', axis=0, tiled=True)  19.6 us
    unnamed x43, local copies, waits for them, and re-layouts  16 us
    all_to_all x1, waiting for transfers between devices, on_device(): lax.all_to_all(image_v, 'seq', split_axis=3, concat_axis=2, tiled=True)  11.2 us
  transfers between devices with their start and end apart: 11, of which 11 were waited for; matrix products, arithmetic and copies ran while one was open for 9% of the time, Pallas kernels for 0%

commit v1 on v0

--- a/solution.py
+++ b/solution.py
@@ -146,7 +146,11 @@
     predicted = jnp.einsum("sti,ic->stc", tok_out[0], out_full, preferred_element_type=jnp.float32)
     residual = predicted - target[0].astype(jnp.float32)
     partial_err = jnp.sum(residual * residual, axis=(1, 2))
-    error_sums = lax.psum(partial_err, "seq")
+    error_sums = partial_err
+    for hop in (1, 2, 4, 8):
+        error_sums = error_sums + lax.ppermute(
+            error_sums, "seq", [(dev, dev ^ hop) for dev in range(16)]
+        )
     mean_errors = error_sums / (seq_len * CH)
     error_gap = mean_errors[0] - ref_errors[0, 0] - (mean_errors[1] - ref_errors[0, 1])
     sigma_t = noise_level(timesteps[0])

time: 487 us -> 469 us (0.963)
  blocking collectives: 33 us -> 0 us
  waiting for transfers between devices: 294 us -> 303 us
  starting transfers between devices: 23.1 us -> 30.3 us
    psum x1 -> x0, blocking collectives: 33 us -> none  [on_device(): error_sums = lax.psum(partial_err, 'seq')]
    ppermute x0 -> x4, waiting for transfers between devices: none -> 7.4 us  [on_device(): lax.ppermute(error_sums, 'seq', [(dev, dev ^ hop) for dev in range(16)])]
    ppermute x0 -> x4, starting transfers between devices: none -> 5.36 us  [on_device(): lax.ppermute(error_sums, 'seq', [(dev, dev ^ hop) for dev in range(16)])]
    unnamed x43 -> x49, local copies, waits for them, and re-layouts: 16 us -> 15.2 us
  transfers between devices with their start and end apart: 11 -> 15, of which waited for: 11 -> 15; matrix products, arithmetic and copies ran while one was open for 9% -> 9% of each run, Pallas kernels for 0% -> 0%
where the time goes in v1:
time: 469 us; the launch traced here: 467 us
  waiting for transfers between devices  303 us (65%)
  matrix products  57.2 us (12%)
  local copies, waits for them, and re-layouts  35.3 us (8%)
  starting transfers between devices  30.3 us (6%)
  other arithmetic  21.4 us (5%)
  between operations  19.8 us (4%)
    all_gather x1, waiting for transfers between devices, on_device(): lax.all_gather(w_in_gate, 'fsdp', axis=0, tiled=True)  59 us
    all_gather x1, waiting for transfers between devices, on_device(): lax.all_gather(w_in_up, 'fsdp', axis=0, tiled=True)  58.3 us
    all_gather x1, waiting for transfers between devices, on_device(): lax.all_gather(w_in_down, 'fsdp', axis=1, tiled=True)  54.7 us
    psum x1, waiting for transfers between devices, on_device(): lax.psum(partial_value.astype(jnp.bfloat16), 'seq').astype(jnp.float32)  50.5 us
    all_gather x1, waiting for transfers between devices, on_device(): lax.all_gather(w_context, 'fsdp', axis=0, tiled=True)  19.6 us
    unnamed x49, local copies, waits for them, and re-layouts  15.2 us
    all_to_all x1, waiting for transfers between devices, on_device(): lax.all_to_all(image_k, 'seq', split_axis=3, concat_axis=2, tiled=True)  11.3 us
    all_to_all x1, waiting for transfers between devices, on_device(): lax.all_to_all(image_v, 'seq', split_axis=3, concat_axis=2, tiled=True)  11.2 us
  transfers between devices with their start and end apart: 15, of which 15 were waited for; matrix products, arithmetic and copies ran while one was open for 9% of the time, Pallas kernels for 0%

profile of v1, /device:TPU:0, one launch (start us, length us, event | category | flops | bytes accessed | tf_op | source)
XLA Modules:
  0.0 467.3 jit_solution(1488441683863711835)
XLA Ops:
  10.0 59.0 %all-gather.6.cloned.1.call-done = bf16[4096,512]{1,0:T(8,128)(2,1)} async-done(((bf16[2048,512]{1,0:T(8,128)(2,1)}), bf16[4096,512]{1,0:T(8,128)(2,1)}) %all-gather.6.cloned.1.call-update) | async-done | bytes 4194320 | tf_op jit(solution)/shard_map/all_gather | solution.py:109
  69.0 3.6 fusion.102
  72.6 54.7 %all-gather.10.cloned.1.call-done = bf16[512,4096]{1,0:T(8,128)(2,1)} async-done(((bf16[512,2048]{1,0:T(8,128)(2,1)}), bf16[512,4096]{1,0:T(8,128)(2,1)}) %all-gather.10.cloned.1.call-update) | async-done | bytes 4194320 | tf_op jit(solution)/shard_map/all_gather | solution.py:111
  127.3 58.3 %all-gather.8.cloned.1.call-done = bf16[4096,512]{1,0:T(8,128)(2,1)} async-done(((bf16[2048,512]{1,0:T(8,128)(2,1)}), bf16[4096,512]{1,0:T(8,128)(2,1)}) %all-gather.8.cloned.1.call-update) | async-done | bytes 4194320 | tf_op jit(solution)/shard_map/all_gather | solution.py:110
  185.6 7.3 %convolution_convert_fusion.2 = bf16[256,4096]{1,0:T(8,128)(2,1)} fusion(bf16[512,4096]{1,0:T(8,128)(2,1)} %all-gather.10.cloned.1.call-done, f32[256,512]{1,0:T(8,128)S(1)} %fusion.102, bf16[4096,512]{1,0:T(8,128)(2,1)} %all-gather.8.cloned.1.call-done, bf16[1,256,4096]{2,1,0:T(8,128)(2,1)S(1)} %copy-done.4, f32[4096]{0:T(1024)S(1)} %copy-done.18, ...), kind=kOutput, calls=%fused_computation.97 | convolution fusion | flops 2152988672 | bytes 13124608 | tf_op jit(solution)/shard_map/dot_general | solution.py:120
  195.4 5.6 %all-to-all-start.2 = ((bf16[16,2,4096]{2,1,0:T(2,128)(2,1)}), bf16[16,2,4096]{2,1,0:T(2,128)(2,1)S(1)}, u32[]{:S(2)}, u32[]{:S(2)}) async-start(bf16[16,2,4096]{2,1,0:T(2,128)(2,1)} %reshape.73), calls=%async_computation.2 | async-start | bytes 524288 | tf_op jit(solution)/shard_map/all_to_all | solution.py:131
  202.5 11.2 %all-to-all-done.2 = bf16[16,2,4096]{2,1,0:T(2,128)(2,1)S(1)} async-done(((bf16[16,2,4096]{2,1,0:T(2,128)(2,1)}), bf16[16,2,4096]{2,1,0:T(2,128)(2,1)S(1)}, u32[]{:S(2)}, u32[]{:S(2)}) %all-to-all-start.2) | async-done | bytes 262176 | tf_op jit(solution)/shard_map/all_to_all | solution.py:131
  213.7 3.5 all-to-all-start.1
  218.8 11.3 %all-to-all-done.1 = bf16[16,2,4096]{2,1,0:T(2,128)(2,1)S(1)} async-done(((bf16[16,2,4096]{2,1,0:T(2,128)(2,1)}), bf16[16,2,4096]{2,1,0:T(2,128)(2,1)S(1)}, u32[]{:S(2)}, u32[]{:S(2)}) %all-to-all-start.1) | async-done | bytes 262176 | tf_op jit(solution)/shard_map/all_to_all | solution.py:130
  230.1 4.2 all-to-all-start
  236.3 2.1 reshape.72
  241.5 4.5 all-to-all-done
  249.0 50.5 %all-reduce.2.cloned.1.call-done = bf16[256,4096]{1,0:T(8,128)(2,1)} async-done(((bf16[256,4096]{1,0:T(8,128)(2,1)}), bf16[256,4096]{1,0:T(8,128)(2,1)}) %all-reduce.2.cloned.1.call-update) | async-done | bytes 2097168 | tf_op jit(solution)/shard_map/psum | solution.py:121
  299.6 2.4 multiply_reduce_fusion
  302.0 19.6 %all-gather.12.cloned.1.call-done = bf16[4096,128]{1,0:T(8,128)(2,1)} async-done(((bf16[2048,128]{1,0:T(8,128)(2,1)}), bf16[4096,128]{1,0:T(8,128)(2,1)}) %all-gather.12.cloned.1.call-update) | async-done | bytes 1048592 | tf_op jit(solution)/shard_map/all_gather | solution.py:112
  321.5 3.0 fusion.91
  325.8 6.9 %while.52 = (s32[]{:T(128)}, bf16[2,512,64]{1,2,0:T(8,128)(2,1)}, bf16[2,512,64]{2,1,0:T(8,128)(2,1)}, bf16[1280,64]{1,0:T(8,128)(2,1)S(1)}, bf16[1280,64]{1,0:T(8,128)(2,1)S(1)}, /*index=5*/s32[]{:T(128)}, s32[]{:T(128)}) while((s32[]{:T(128)}, bf16[2,512,64]{1,2,0:T(8,128)(2,1)}, bf16[2,512,64]{2,1,0:T(8,128)(2,1)}, ...), condition=%wide.region_6.7_spmd.clone, body=%wide.region_3.6_spmd.clone.sunk | while | flops 173048064 | bytes 8402513 | solution.py:45
  333.9 3.9 while.53
  339.6 5.6 %all-to-all-start.3 = ((bf16[16,2,4096]{2,1,0:T(2,128)(2,1)}), bf16[16,2,4096]{2,1,0:T(2,128)(2,1)S(1)}, u32[]{:S(2)}, u32[]{:S(2)}) async-start(bf16[16,2,4096]{2,1,0:T(2,128)(2,1)} %reshape.75), calls=%async_computation.3 | async-start | bytes 524288 | tf_op jit(solution)/shard_map/all_to_all | solution.py:145
  346.6 8.7 %all-to-all-done.3 = bf16[16,2,4096]{2,1,0:T(2,128)(2,1)S(1)} async-done(((bf16[16,2,4096]{2,1,0:T(2,128)(2,1)}), bf16[16,2,4096]{2,1,0:T(2,128)(2,1)S(1)}, u32[]{:S(2)}, u32[]{:S(2)}) %all-to-all-start.3) | async-done | bytes 262176 | tf_op jit(solution)/shard_map/all_to_all | solution.py:145
  357.0 5.0 %all-gather.14.cloned.1.call-done = bf16[1024,1280]{1,0:T(8,128)(2,1)} async-done(((bf16[512,1280]{1,0:T(8,128)(2,1)}), bf16[1024,1280]{1,0:T(8,128)(2,1)}) %all-gather.14.cloned.1.call-update) | async-done | bytes 2621456 | tf_op jit(solution)/shard_map/all_gather | solution.py:113
  362.0 3.4 multiply_reduce_fusion.1
  368.0 2.1 collective-permute-done.1
  371.6 2.1 collective-permute-done.2
  373.6 2.4 collective-permute-start.3
  376.0 2.1 collective-permute-done.3
  381.4 2.8 fusion.88
  386.6 5.6 %all-to-all-start.4 = ((bf16[16,2,4096]{2,1,0:T(2,128)(2,1)}), bf16[16,2,4096]{2,1,0:T(2,128)(2,1)S(1)}, u32[]{:S(2)}, u32[]{:S(2)}) async-start(bf16[16,2,4096]{2,1,0:T(2,128)(2,1)} %reshape.77), calls=%async_computation.4 | async-start | bytes 524288 | tf_op jit(solution)/shard_map/all_to_all | solution.py:165
  392.3 9.9 %all-to-all-done.4 = bf16[16,2,4096]{2,1,0:T(2,128)(2,1)S(1)} async-done(((bf16[16,2,4096]{2,1,0:T(2,128)(2,1)}), bf16[16,2,4096]{2,1,0:T(2,128)(2,1)S(1)}, u32[]{:S(2)}, u32[]{:S(2)}) %all-to-all-start.4) | async-done | bytes 262176 | tf_op jit(solution)/shard_map/all_to_all | solution.py:165
  405.4 22.8 %while.54 = (s32[]{:T(128)}, f32[1024,64]{0,1:T(8,128)}, f32[1024,64]{0,1:T(8,128)}, bf16[2,512,64]{1,2,0:T(8,128)(2,1)}, bf16[2,512,64]{2,1,0:T(8,128)(2,1)}, /...) while((s32[]{:T(128)}, f32[1024,64]{0,1:T(8,128)}, ...), condition=%wide.region_16.17_spmd.clone, body=%wide.region_12.16_spmd.clone.sunk | while | flops 394821376 | bytes 17910924 | solution.py:83
  422.9 2.1 convolution_add_fusion.8
  432.2 18.9 %while.55 = (s32[]{:T(128)}, f32[1024,64]{0,1:T(8,128)}, f32[1024,64]{0,1:T(8,128)}, bf16[2,512,64]{1,2,0:T(8,128)(2,1)}, bf16[2,512,64]{2,1,0:T(8,128)(2,1)S(1)...) while((s32[]{:T(128)}, f32[1024,64]{0,1:T(8,128)}, ...), condition=%wide.region_21.22_spmd.clone, body=%wide.region_17.21_spmd.clone.sunk | while | flops 394821376 | bytes 21187588 | solution.py:83
  (191 shorter events, 94.8 us)
Async XLA Ops:
  7.2 2.3 copy-start.4
  7.2 61.8 %all-gather.6.cloned.1.call-start = ((), (), s32[]{:S(2)}) async-start(), calls=%async_computation.5 | async-start | bytes 6291456 | tf_op jit(solution)/shard_map/all_gather | solution.py:109
  7.9 119.4 %all-gather.10.cloned.1.call-start = ((), (), s32[]{:S(2)}) async-start(), calls=%async_computation.7 | async-start | bytes 6291456 | tf_op jit(solution)/shard_map/all_gather | solution.py:111
  8.7 60.4 %copy-start.18 = (f32[4096]{0:T(1024)S(1)}, f32[4096]{0:T(1024)}, u32[]{:S(2)}) copy-start(f32[4096]{0:T(1024)} %param.27) | copy-start | bytes 49156
  8.7 176.9 %all-gather.8.cloned.1.call-start = ((), (), s32[]{:S(2)}) async-start(), calls=%async_computation.6 | async-start | bytes 6291456 | tf_op jit(solution)/shard_map/all_gather | solution.py:110
  9.4 290.1 %all-reduce.2.cloned.1.call-start = ((), (), s32[]{:S(2)}) async-start(), calls=%async_computation.8 | async-start | bytes 4194304 | tf_op jit(solution)/shard_map/psum | solution.py:121
  193.0 8.1 %copy-start.13 = (bf16[1,2,64,1024]{3,2,1,0:T(8,128)(2,1)S(1)}, bf16[1,2,64,1024]{3,2,1,0:T(8,128)(2,1)}, u32[]{:S(2)}) copy-start(bf16[1,2,64,1024]{3,2,1,0:T(8,128)(2,1)} %param.34) | copy-start | bytes 786436
  193.0 24.3 %copy-start.14 = (bf16[1,2,64,1024]{3,2,1,0:T(8,128)(2,1)S(1)}, bf16[1,2,64,1024]{3,2,1,0:T(8,128)(2,1)}, u32[]{:S(2)}) copy-start(bf16[1,2,64,1024]{3,2,1,0:T(8,128)(2,1)} %param.33) | copy-start | bytes 786436
  193.0 128.5 %all-gather.12.cloned.1.call-start = ((), (), s32[]{:S(2)}) async-start(), calls=%async_computation.9 | async-start | bytes 1572864 | tf_op jit(solution)/shard_map/all_gather | solution.py:112
  195.4 18.3 %all-to-all-start.2 = ((bf16[16,2,4096]{2,1,0:T(2,128)(2,1)}), bf16[16,2,4096]{2,1,0:T(2,128)(2,1)S(1)}, u32[]{:S(2)}, u32[]{:S(2)}) async-start(bf16[16,2,4096]{2,1,0:T(2,128)(2,1)} %reshape.73), calls=%async_computation.2 | async-start | bytes 524288 | tf_op jit(solution)/shard_map/all_to_all | solution.py:131
  213.7 16.3 %all-to-all-start.1 = ((bf16[16,2,4096]{2,1,0:T(2,128)(2,1)}), bf16[16,2,4096]{2,1,0:T(2,128)(2,1)S(1)}, u32[]{:S(2)}, u32[]{:S(2)}) async-start(bf16[16,2,4096]{2,1,0:T(2,128)(2,1)} %reshape.71), calls=%async_computation.1 | async-start | bytes 524288 | tf_op jit(solution)/shard_map/all_to_all | solution.py:130
  230.1 5.4 %copy-start.7 = (bf16[16,2,4096]{2,1,0:T(2,128)(2,1)}, bf16[16,2,4096]{2,1,0:T(2,128)(2,1)S(1)}, u32[]{:S(2)}) copy-start(bf16[16,2,4096]{2,1,0:T(2,128)(2,1)S(1)} %all-to-all-done.1) | copy-start | bytes 786436
  230.1 15.9 %all-to-all-start = ((bf16[16,2,4096]{2,1,0:T(2,128)(2,1)}), bf16[16,2,4096]{2,1,0:T(2,128)(2,1)}, u32[]{:S(2)}, u32[]{:S(2)}) async-start(bf16[16,2,4096]{2,1,0:T(2,128)(2,1)} %reshape.69), calls=%async_computation | async-start | bytes 524288 | tf_op jit(solution)/shard_map/all_to_all | solution.py:129
  234.3 127.7 %all-gather.14.cloned.1.call-start = ((), (), s32[]{:S(2)}) async-start(), calls=%async_computation.10 | async-start | bytes 3932160 | tf_op jit(solution)/shard_map/all_gather | solution.py:113
  248.0 73.5 %copy-start.19 = (f32[4096]{0:T(1024)S(1)}, f32[4096]{0:T(1024)}, u32[]{:S(2)}) copy-start(f32[4096]{0:T(1024)} %param.31) | copy-start | bytes 49156
  301.9 22.9 %copy-start.8 = (bf16[1024,64]{1,0:T(8,128)(2,1)S(1)}, bf16[1024,64]{1,0:T(8,128)(2,1)}, u32[]{:S(2)}) copy-start(bf16[1024,64]{1,0:T(8,128)(2,1)} %get-tuple-element.450) | copy-start | bytes 393220
  301.9 22.9 %copy-start.9 = (bf16[1024,64]{1,0:T(8,128)(2,1)S(1)}, bf16[1024,64]{1,0:T(8,128)(2,1)}, u32[]{:S(2)}) copy-start(bf16[1024,64]{1,0:T(8,128)(2,1)} %get-tuple-element.451) | copy-start | bytes 393220
  301.9 22.9 %copy-start.10 = (bf16[1024,64]{1,0:T(8,128)(2,1)S(1)}, bf16[1024,64]{1,0:T(8,128)(2,1)}, u32[]{:S(2)}) copy-start(bf16[1024,64]{1,0:T(8,128)(2,1)} %get-tuple-element.452) | copy-start | bytes 393220
  301.9 22.9 %copy-start.11 = (bf16[1024,64]{1,0:T(8,128)(2,1)S(1)}, bf16[1024,64]{1,0:T(8,128)(2,1)}, u32[]{:S(2)}) copy-start(bf16[1024,64]{1,0:T(8,128)(2,1)} %get-tuple-element.453) | copy-start | bytes 393220
  337.8 19.2 %copy-start.1 = (bf16[1280,64]{1,0:T(8,128)(2,1)}, bf16[1280,64]{1,0:T(8,128)(2,1)S(1)}, u32[]{:S(2)}) copy-start(bf16[1280,64]{1,0:T(8,128)(2,1)S(1)} %get-tuple-element.807) | copy-start | bytes 491524
  337.8 19.2 %copy-start.5 = (bf16[2,512,64]{1,2,0:T(8,128)(2,1)}, bf16[2,512,64]{1,2,0:T(8,128)(2,1)S(1)}, u32[]{:S(2)}) copy-start(bf16[2,512,64]{1,2,0:T(8,128)(2,1)S(1)} %get-tuple-element.734) | copy-start | bytes 393220
  337.8 8.1 %copy-start.17 = (f32[1,2]{1,0:T(1,128)S(1)}, f32[1,2]{1,0:T(1,128)}, u32[]{:S(2)}) copy-start(f32[1,2]{1,0:T(1,128)} %param.26) | copy-start | bytes 28
  339.6 15.6 %all-to-all-start.3 = ((bf16[16,2,4096]{2,1,0:T(2,128)(2,1)}), bf16[16,2,4096]{2,1,0:T(2,128)(2,1)S(1)}, u32[]{:S(2)}, u32[]{:S(2)}) async-start(bf16[16,2,4096]{2,1,0:T(2,128)(2,1)} %reshape.75), calls=%async_computation.3 | async-start | bytes 524288 | tf_op jit(solution)/shard_map/all_to_all | solution.py:145
  362.0 19.5 %copy-start = (bf16[1024,1280]{1,0:T(8,128)(2,1)S(1)}, bf16[1024,1280]{1,0:T(8,128)(2,1)}, u32[]{:S(2)}) copy-start(bf16[1024,1280]{1,0:T(8,128)(2,1)} %all-gather.14.cloned.1.call-done) | copy-start | bytes 7864324
  365.3 1.2 collective-permute-start
  366.5 3.6 collective-permute-start.1
  370.1 3.6 collective-permute-start.2
  373.6 4.5 collective-permute-start.3
  386.6 15.6 %all-to-all-start.4 = ((bf16[16,2,4096]{2,1,0:T(2,128)(2,1)}), bf16[16,2,4096]{2,1,0:T(2,128)(2,1)S(1)}, u32[]{:S(2)}, u32[]{:S(2)}) async-start(bf16[16,2,4096]{2,1,0:T(2,128)(2,1)} %reshape.77), calls=%async_computation.4 | async-start | bytes 524288 | tf_op jit(solution)/shard_map/all_to_all | solution.py:165
  433.4 2.1 copy-start.2
  437.0 2.2 copy-start.15
  445.9 3.2 copy-start.15
  (7 other events, 7.5 us)
Sparse Core Ops, SparseCore 0:
  9.5 59.4 all-gather.5
  70.5 56.7 all-gather.9
  128.9 56.7 all-gather.7
  193.1 106.4 all-reduce.1
  300.9 20.5 all-gather.11
  322.9 38.9 all-gather.13
